TPU v7x, 32 devices: a whole 2x2x4 slice. The times are simulated.
32 devices in a mesh: band: 4 (over y, x), query: 8 (over z, core).
Axes of the slice: x: 2, y: 2, z: 4, core: 2. Of those that a mesh axis runs over, the one named last changes fastest.
Arguments:
- spectra: bfloat16 [192, 20480], P('band'), may hold values from 0 to 3
- theo: bfloat16 [8, 8, 20480], P('query', 'band'), may hold values from -0.0390625 to 0.0390625
- offsets: int32 [16], replicated, may hold values from -128 to 128
- win_lo: int32 [192], P('band'), may hold values from 0 to 32
- win_len: int32 [192], P('band'), may hold values from 1 to 32
Outputs:
- best: float32 [192, 16], P(('band', 'query'))
- average: float32 [192, 16], P(('band', 'query'))
Inputs may be any that keep to these rules, and one draw needn't show every extreme that they name: win_lo + win_len never exceeds 64.
All inputs are finite; a program needn't handle non-finite values.
Results may differ from a plain program's by a relative error of at most 0.003.
Values may be sent and summed in bfloat16 or wider, within the bound.
A program may use at most 128 MiB of HBM per device.

v0:
```python
import jax
import jax.numpy as jnp
from jax import lax
from jax.sharding import PartitionSpec as P

BG_HALF = 75
SHIFT_MAX = 128


def box_table():
    source = lax.broadcasted_iota(jnp.int32, (384, 128), 0)
    target = lax.broadcasted_iota(jnp.int32, (384, 128), 1)
    offset_gap = source - 128 - target
    inside = (jnp.abs(offset_gap) <= BG_HALF) & (offset_gap != 0)
    return inside.astype(jnp.bfloat16)


def correct(intensity):
    row_count, bin_count = intensity.shape
    block_count = bin_count // 128
    blocks = intensity.reshape(row_count, block_count, 128)
    zero_block = jnp.zeros((row_count, 1, 128), intensity.dtype)
    previous = jnp.concatenate([zero_block, blocks[:, :-1]], axis=1)
    following = jnp.concatenate([blocks[:, 1:], zero_block], axis=1)
    stacked = jnp.concatenate([previous, blocks, following], axis=2)
    window_sum = jnp.einsum("rbj,ji->rbi", stacked, box_table(), preferred_element_type=jnp.float32)
    result = blocks.astype(jnp.float32) - window_sum / (2.0 * BG_HALF)
    return result.astype(jnp.bfloat16).reshape(row_count, bin_count)


def shifted_copies(peptides, offsets):
    bin_count = peptides.shape[1]
    padded = jnp.pad(peptides, ((0, 0), (SHIFT_MAX, SHIFT_MAX)))

    def take_shift(offset):
        return lax.dynamic_slice_in_dim(padded, SHIFT_MAX - offset, bin_count, 1)

    copies = jax.vmap(take_shift, out_axes=1)(offsets)
    return copies.reshape(-1, bin_count)


def local(spectra, theo, offsets, win_lo, win_len):
    query_count = lax.axis_size("query")
    spectra_rows = spectra.shape[0]
    own_rows = spectra_rows // query_count
    own_start = lax.axis_index("query") * own_rows
    corrected = correct(spectra)
    shift_count = offsets.shape[0]
    group_size = theo.shape[1] * lax.axis_size("band")
    piece = lax.all_gather(theo, "band", axis=1, tiled=True)
    piece_rows = piece.shape[1]
    copies = shifted_copies(piece[0], offsets)
    partial_scores = jnp.einsum("mb,sb->ms", copies, corrected, preferred_element_type=jnp.float32)
    scores = partial_scores.reshape(1, piece_rows, shift_count * spectra_rows)
    score_table = scores.reshape(group_size, shift_count, query_count, own_rows)
    low_own = lax.dynamic_slice_in_dim(win_lo, own_start, own_rows, 0)
    length_own = lax.dynamic_slice_in_dim(win_len, own_start, own_rows, 0)
    gathered = lax.all_to_all(score_table, "query", split_axis=2, concat_axis=0, tiled=True)
    total_peptides = gathered.shape[0]
    owned_scores = gathered.reshape(total_peptides, shift_count, own_rows)
    peptide_index = lax.broadcasted_iota(jnp.int32, (total_peptides, own_rows), 0)
    inside = (peptide_index >= low_own[None, :]) & (peptide_index < (low_own + length_own)[None, :])
    best_score = jnp.max(jnp.where(inside[:, None, :], owned_scores, -jnp.inf), axis=0).T
    totals = jnp.sum(jnp.where(inside[:, None, :], owned_scores, 0.0), axis=0).T
    average = totals / length_own[:, None].astype(jnp.float32)
    return (best_score, average)


def solution(mesh):
    placed = (P("band", None), P("query", "band", None), P(), P("band"), P("band"))
    return jax.shard_map(
        local,
        mesh=mesh,
        in_specs=placed,
        out_specs=(P(("band", "query"), None), P(("band", "query"), None)),
        check_vma=False,
    )
```

profile of v0, /device:TPU:0, one launch (start us, length us, event | category | flops | bytes accessed | tf_op | source)
XLA Modules:
  0.0 84.9 jit_solution(6701654885838280901)
XLA Ops:
  0.7 1.2 %copy.17 = bf16[1,2,20480]{2,0,1:T(2,128)(2,1)S(1)} copy(bf16[1,2,20480]{2,1,0:T(2,128)(2,1)} %param.6) | data formatting | bytes 163840 | tf_op args[1]
  1.8 12.0 %all_gather.3 = bf16[1,8,20480]{2,0,1:T(2,128)(2,1)S(1)} all-gather(bf16[1,2,20480]{2,0,1:T(2,128)(2,1)S(1)} %copy.17), channel_id=1, replica_groups=mesh['band'=4,'query'=8] {'band'}, dimensions={1}, use_global_device_ids=true | all-gather | bytes 409600 | tf_op jit(solution)/shard_map/all_gather | solution.py:50
  13.8 0.4 copy.28
  14.2 0.7 fusion.29
  14.9 34.0 %while.1 = (s32[]{:T(128)}, bf16[8,20736]{1,0:T(8,128)(2,1)S(1)}, s32[16,2]{0,1:T(2,128)S(1)}, bf16[16,8,20480]{2,1,0:T(8,128)(2,1)}, s32[]{:T(128)}) while((s32[]{:T(128)}, bf16[8,20736]{1,0:T(8,128)(2,1)S(1)}, s32[16,2]{0,1:T(2,128)S(1)}, bf16[16,8,20480]{2,1,0:T(8,128)(2,1)}, s32[]{:T(128)}) %tuple.24), condition=%wide.while_cond, body=%wide.while_body.sunk | while | flops 2 | bytes 655973 | solution.py:36
  14.9 0.1 constant_dynamic-slice_fusion.2
  15.0 0.5 slice.24
  15.5 1.5 %bitcast_dynamic-update-slice_fusion.2 = bf16[16,8,20480]{2,1,0:T(8,128)(2,1)} fusion(bf16[16,8,20480]{2,1,0:T(8,128)(2,1)} %get-tuple-element.58, s32[]{:T(128)S(6)} %copy.32, bf16[8,20736]{1,0:T(8,128)(2,1)S(1)} %get-tuple-element.61, s32[]{:T(128)} %bitcast.41), kind=kLoop, calls=%fused_computation.clone.1 | loop fusion | bytes 655876 | tf_op jit(solution)/shard_map/vmap()/gather
  17.0 0.1 constant_dynamic-slice_fusion.2
  17.1 0.5 slice.24
  17.6 1.5 %bitcast_dynamic-update-slice_fusion.2 = bf16[16,8,20480]{2,1,0:T(8,128)(2,1)} fusion(bf16[16,8,20480]{2,1,0:T(8,128)(2,1)} %get-tuple-element.58, s32[]{:T(128)S(6)} %copy.32, bf16[8,20736]{1,0:T(8,128)(2,1)S(1)} %get-tuple-element.61, s32[]{:T(128)} %bitcast.41), kind=kLoop, calls=%fused_computation.clone.1 | loop fusion | bytes 655876 | tf_op jit(solution)/shard_map/vmap()/gather
  19.2 0.1 constant_dynamic-slice_fusion.2
  19.2 0.5 slice.24
  19.8 1.5 %bitcast_dynamic-update-slice_fusion.2 = bf16[16,8,20480]{2,1,0:T(8,128)(2,1)} fusion(bf16[16,8,20480]{2,1,0:T(8,128)(2,1)} %get-tuple-element.58, s32[]{:T(128)S(6)} %copy.32, bf16[8,20736]{1,0:T(8,128)(2,1)S(1)} %get-tuple-element.61, s32[]{:T(128)} %bitcast.41), kind=kLoop, calls=%fused_computation.clone.1 | loop fusion | bytes 655876 | tf_op jit(solution)/shard_map/vmap()/gather
  21.3 0.1 constant_dynamic-slice_fusion.2
  21.4 0.5 slice.24
  21.9 1.5 %bitcast_dynamic-update-slice_fusion.2 = bf16[16,8,20480]{2,1,0:T(8,128)(2,1)} fusion(bf16[16,8,20480]{2,1,0:T(8,128)(2,1)} %get-tuple-element.58, s32[]{:T(128)S(6)} %copy.32, bf16[8,20736]{1,0:T(8,128)(2,1)S(1)} %get-tuple-element.61, s32[]{:T(128)} %bitcast.41), kind=kLoop, calls=%fused_computation.clone.1 | loop fusion | bytes 655876 | tf_op jit(solution)/shard_map/vmap()/gather
  23.4 0.1 constant_dynamic-slice_fusion.2
  23.5 0.5 slice.24
  24.0 1.5 %bitcast_dynamic-update-slice_fusion.2 = bf16[16,8,20480]{2,1,0:T(8,128)(2,1)} fusion(bf16[16,8,20480]{2,1,0:T(8,128)(2,1)} %get-tuple-element.58, s32[]{:T(128)S(6)} %copy.32, bf16[8,20736]{1,0:T(8,128)(2,1)S(1)} %get-tuple-element.61, s32[]{:T(128)} %bitcast.41), kind=kLoop, calls=%fused_computation.clone.1 | loop fusion | bytes 655876 | tf_op jit(solution)/shard_map/vmap()/gather
  25.5 0.1 constant_dynamic-slice_fusion.2
  25.6 0.5 slice.24
  26.1 1.5 %bitcast_dynamic-update-slice_fusion.2 = bf16[16,8,20480]{2,1,0:T(8,128)(2,1)} fusion(bf16[16,8,20480]{2,1,0:T(8,128)(2,1)} %get-tuple-element.58, s32[]{:T(128)S(6)} %copy.32, bf16[8,20736]{1,0:T(8,128)(2,1)S(1)} %get-tuple-element.61, s32[]{:T(128)} %bitcast.41), kind=kLoop, calls=%fused_computation.clone.1 | loop fusion | bytes 655876 | tf_op jit(solution)/shard_map/vmap()/gather
  27.7 0.1 constant_dynamic-slice_fusion.2
  27.7 0.5 slice.24
  28.2 1.6 %bitcast_dynamic-update-slice_fusion.2 = bf16[16,8,20480]{2,1,0:T(8,128)(2,1)} fusion(bf16[16,8,20480]{2,1,0:T(8,128)(2,1)} %get-tuple-element.58, s32[]{:T(128)S(6)} %copy.32, bf16[8,20736]{1,0:T(8,128)(2,1)S(1)} %get-tuple-element.61, s32[]{:T(128)} %bitcast.41), kind=kLoop, calls=%fused_computation.clone.1 | loop fusion | bytes 655876 | tf_op jit(solution)/shard_map/vmap()/gather
  29.8 0.1 constant_dynamic-slice_fusion.2
  29.9 0.5 slice.24
  30.4 1.5 %bitcast_dynamic-update-slice_fusion.2 = bf16[16,8,20480]{2,1,0:T(8,128)(2,1)} fusion(bf16[16,8,20480]{2,1,0:T(8,128)(2,1)} %get-tuple-element.58, s32[]{:T(128)S(6)} %copy.32, bf16[8,20736]{1,0:T(8,128)(2,1)S(1)} %get-tuple-element.61, s32[]{:T(128)} %bitcast.41), kind=kLoop, calls=%fused_computation.clone.1 | loop fusion | bytes 655876 | tf_op jit(solution)/shard_map/vmap()/gather
  31.9 0.1 constant_dynamic-slice_fusion.2
  32.0 0.5 slice.24
  32.5 1.5 %bitcast_dynamic-update-slice_fusion.2 = bf16[16,8,20480]{2,1,0:T(8,128)(2,1)} fusion(bf16[16,8,20480]{2,1,0:T(8,128)(2,1)} %get-tuple-element.58, s32[]{:T(128)S(6)} %copy.32, bf16[8,20736]{1,0:T(8,128)(2,1)S(1)} %get-tuple-element.61, s32[]{:T(128)} %bitcast.41), kind=kLoop, calls=%fused_computation.clone.1 | loop fusion | bytes 655876 | tf_op jit(solution)/shard_map/vmap()/gather
  34.0 0.1 constant_dynamic-slice_fusion.2
  34.1 0.5 slice.24
  34.6 1.5 %bitcast_dynamic-update-slice_fusion.2 = bf16[16,8,20480]{2,1,0:T(8,128)(2,1)} fusion(bf16[16,8,20480]{2,1,0:T(8,128)(2,1)} %get-tuple-element.58, s32[]{:T(128)S(6)} %copy.32, bf16[8,20736]{1,0:T(8,128)(2,1)S(1)} %get-tuple-element.61, s32[]{:T(128)} %bitcast.41), kind=kLoop, calls=%fused_computation.clone.1 | loop fusion | bytes 655876 | tf_op jit(solution)/shard_map/vmap()/gather
  36.2 0.1 constant_dynamic-slice_fusion.2
  36.2 0.5 slice.24
  36.8 1.5 %bitcast_dynamic-update-slice_fusion.2 = bf16[16,8,20480]{2,1,0:T(8,128)(2,1)} fusion(bf16[16,8,20480]{2,1,0:T(8,128)(2,1)} %get-tuple-element.58, s32[]{:T(128)S(6)} %copy.32, bf16[8,20736]{1,0:T(8,128)(2,1)S(1)} %get-tuple-element.61, s32[]{:T(128)} %bitcast.41), kind=kLoop, calls=%fused_computation.clone.1 | loop fusion | bytes 655876 | tf_op jit(solution)/shard_map/vmap()/gather
  38.4 0.5 slice.24
  38.9 1.5 %bitcast_dynamic-update-slice_fusion.2 = bf16[16,8,20480]{2,1,0:T(8,128)(2,1)} fusion(bf16[16,8,20480]{2,1,0:T(8,128)(2,1)} %get-tuple-element.58, s32[]{:T(128)S(6)} %copy.32, bf16[8,20736]{1,0:T(8,128)(2,1)S(1)} %get-tuple-element.61, s32[]{:T(128)} %bitcast.41), kind=kLoop, calls=%fused_computation.clone.1 | loop fusion | bytes 655876 | tf_op jit(solution)/shard_map/vmap()/gather
  40.5 0.5 slice.24
  41.0 1.5 %bitcast_dynamic-update-slice_fusion.2 = bf16[16,8,20480]{2,1,0:T(8,128)(2,1)} fusion(bf16[16,8,20480]{2,1,0:T(8,128)(2,1)} %get-tuple-element.58, s32[]{:T(128)S(6)} %copy.32, bf16[8,20736]{1,0:T(8,128)(2,1)S(1)} %get-tuple-element.61, s32[]{:T(128)} %bitcast.41), kind=kLoop, calls=%fused_computation.clone.1 | loop fusion | bytes 655876 | tf_op jit(solution)/shard_map/vmap()/gather
  42.6 0.5 slice.24
  43.1 1.5 %bitcast_dynamic-update-slice_fusion.2 = bf16[16,8,20480]{2,1,0:T(8,128)(2,1)} fusion(bf16[16,8,20480]{2,1,0:T(8,128)(2,1)} %get-tuple-element.58, s32[]{:T(128)S(6)} %copy.32, bf16[8,20736]{1,0:T(8,128)(2,1)S(1)} %get-tuple-element.61, s32[]{:T(128)} %bitcast.41), kind=kLoop, calls=%fused_computation.clone.1 | loop fusion | bytes 655876 | tf_op jit(solution)/shard_map/vmap()/gather
  44.7 0.5 slice.24
  45.2 1.5 %bitcast_dynamic-update-slice_fusion.2 = bf16[16,8,20480]{2,1,0:T(8,128)(2,1)} fusion(bf16[16,8,20480]{2,1,0:T(8,128)(2,1)} %get-tuple-element.58, s32[]{:T(128)S(6)} %copy.32, bf16[8,20736]{1,0:T(8,128)(2,1)S(1)} %get-tuple-element.61, s32[]{:T(128)} %bitcast.41), kind=kLoop, calls=%fused_computation.clone.1 | loop fusion | bytes 655876 | tf_op jit(solution)/shard_map/vmap()/gather
  46.8 0.5 slice.24
  47.3 1.5 %bitcast_dynamic-update-slice_fusion.2 = bf16[16,8,20480]{2,1,0:T(8,128)(2,1)} fusion(bf16[16,8,20480]{2,1,0:T(8,128)(2,1)} %get-tuple-element.58, s32[]{:T(128)S(6)} %copy.32, bf16[8,20736]{1,0:T(8,128)(2,1)S(1)} %get-tuple-element.61, s32[]{:T(128)} %bitcast.41), kind=kLoop, calls=%fused_computation.clone.1 | loop fusion | bytes 655876 | tf_op jit(solution)/shard_map/vmap()/gather
  48.9 0.3 copy.22
  49.2 1.2 %fusion.36 = (bf16[48,159,128]{2,1,0:T(8,128)(2,1)S(1)}, bf16[48,159,128]{2,1,0:T(8,128)(2,1)S(1)}) fusion(bf16[48,160,128]{2,1,0:T(8,128)(2,1)S(1)} %bitcast.42), kind=kLoop, calls=%fused_computation.47 | loop fusion | bytes 7815168 | tf_op jit(solution)/shard_map/slice | solution.py:23
  50.4 3.1 %subtract_convert_fusion = bf16[48,160,128]{2,1,0:T(8,128)(2,1)} fusion(bf16[48,160,128]{2,1,0:T(8,128)(2,1)S(1)} %bitcast.43, bf16[48,159,128]{2,1,0:T(8,128)(2,1)S(1)} %get-tuple-element.23, bf16[48,159,128]{2,1,0:T(8,128)(2,1)S(1)} %get-tuple-element.22, s32[384]{0:T(512)S(1)} %iota_add_fusion), kind=kOutput, calls=%fused_computation.16 | convolution fusion | flops 788643840 | bytes 7841280 | tf_op jit(solution)/shard_map/rbj,ji->rbi/dot_general | solution.py:26
  53.5 3.7 %dot_general.9 = bf16[8,6,20480]{2,1,0:T(8,128)(2,1)S(1)} reshape(bf16[48,160,128]{2,1,0:T(8,128)(2,1)} %subtract_convert_fusion) | data formatting | bytes 3932160 | tf_op jit(solution)/shard_map/mb,sb->ms/dot_general | solution.py:53
  57.3 13.3 %fusion.12 = f32[8,16,8,6]{2,0,3,1:T(8,128)S(1)} fusion(bf16[16,8,20480]{2,1,0:T(8,128)(2,1)} %get-tuple-element.9, bf16[8,6,20480]{2,1,0:T(8,128)(2,1)S(1)} %dot_general.9), kind=kOutput, calls=%fused_computation.14 | convolution fusion | flops 251658240 | bytes 7233536 | tf_op jit(solution)/shard_map/mb,sb->ms/dot_general | solution.py:53
  70.6 0.2 copy.19
  70.8 0.7 reshape.74
  71.6 4.9 %all-to-all-start = ((f32[8,1,768]{2,1,0:T(1,128)}), f32[8,1,768]{2,1,0:T(1,128)S(1)}, u32[]{:S(2)}, u32[]{:S(2)}) async-start(f32[8,1,768]{2,1,0:T(1,128)} %reshape.74), calls=%async_computation | async-start | bytes 49152 | tf_op jit(solution)/shard_map/all_to_all | solution.py:58
  76.5 0.1 dynamic-slice_add_fusion
  76.6 0.1 compare_and_fusion
  76.6 5.5 %all-to-all-done = f32[8,1,768]{2,1,0:T(1,128)S(1)} async-done(((f32[8,1,768]{2,1,0:T(1,128)}), f32[8,1,768]{2,1,0:T(1,128)S(1)}, u32[]{:S(2)}, u32[]{:S(2)}) %all-to-all-start) | async-done | bytes 24608 | tf_op jit(solution)/shard_map/all_to_all | solution.py:58
  82.2 0.5 broadcast.91
  82.7 0.7 reduce.2
  83.4 0.1 reshape.75
  83.5 0.7 fusion.20
  84.2 0.7 divide_bitcast_fusion
  (16 shorter events, 0.4 us)
Async XLA Ops:
  0.6 48.3 %copy-start = (bf16[48,20480]{1,0:T(8,128)(2,1)S(1)}, bf16[48,20480]{1,0:T(8,128)(2,1)}, u32[]{:S(2)}) copy-start(bf16[48,20480]{1,0:T(8,128)(2,1)} %param.5) | copy-start | bytes 5898244
  57.2 19.2 %copy-start.1 = (s32[48]{0:T(128)S(1)}, s32[48]{0:T(128)}, u32[]{:S(2)}) copy-start(s32[48]{0:T(128)} %param.9) | copy-start | bytes 580
  57.3 19.2 %copy-start.2 = (s32[48]{0:T(128)S(1)}, s32[48]{0:T(128)}, u32[]{:S(2)}) copy-start(s32[48]{0:T(128)} %param.8) | copy-start | bytes 580
  71.6 10.6 %all-to-all-start = ((f32[8,1,768]{2,1,0:T(1,128)}), f32[8,1,768]{2,1,0:T(1,128)S(1)}, u32[]{:S(2)}, u32[]{:S(2)}) async-start(f32[8,1,768]{2,1,0:T(1,128)} %reshape.74), calls=%async_computation | async-start | bytes 49152 | tf_op jit(solution)/shard_map/all_to_all | solution.py:58
where the time goes:
time: 85.3 us; the launch traced here: 84.9 us
  local copies, waits for them, and re-layouts  42.3 us (50%)
  matrix products  16.4 us (19%)
  blocking collectives  12 us (14%)
  waiting for transfers between devices  5.51 us (6%)
  starting transfers between devices  4.88 us (6%)
  other arithmetic  2.93 us (3%)
    gather x48, local copies, waits for them, and re-layouts  33.9 us
    dot_general x1, matrix products, local(): jnp.einsum('mb,sb->ms', copies, corrected, preferred_element_type=jnp.flo...  13.3 us
    all_gather x1, blocking collectives, local(): piece = lax.all_gather(theo, 'band', axis=1, tiled=True)  12 us
    all_to_all x1, waiting for transfers between devices, local(): lax.all_to_all(score_table, 'query', split_axis=2, concat_axis=0, tiled=T...  5.51 us
    all_to_all x1, starting transfers between devices, local(): lax.all_to_all(score_table, 'query', split_axis=2, concat_axis=0, tiled=T...  4.88 us
    dot_general x2, local copies, waits for them, and re-layouts, local(): jnp.einsum('mb,sb->ms', copies, corrected, preferred_element_type=jnp.flo...  3.95 us
    dot_general x1, matrix products, correct(): jnp.einsum('rbj,ji->rbi', stacked, box_table(), preferred_element_type=jn...  3.08 us
    unnamed x11, local copies, waits for them, and re-layouts  2.71 us
  transfers between devices with their start and end apart: 1, of which 1 were waited for; matrix products, arithmetic and copies ran while one was open for 0% of the time, Pallas kernels for 0%

commit v1 on v0

--- a/solution.py
+++ b/solution.py
@@ -55,7 +55,10 @@
     score_table = scores.reshape(group_size, shift_count, query_count, own_rows)
     low_own = lax.dynamic_slice_in_dim(win_lo, own_start, own_rows, 0)
     length_own = lax.dynamic_slice_in_dim(win_len, own_start, own_rows, 0)
-    gathered = lax.all_to_all(score_table, "query", split_axis=2, concat_axis=0, tiled=True)
+    count = lax.axis_size("query")
+    tiles = jnp.stack(jnp.split(score_table, count, axis=2), axis=0)
+    tiles = lax.all_to_all(tiles, "query", split_axis=0, concat_axis=0)
+    gathered = jnp.concatenate(tiles, axis=0)
     total_peptides = gathered.shape[0]
     owned_scores = gathered.reshape(total_peptides, shift_count, own_rows)
     peptide_index = lax.broadcasted_iota(jnp.int32, (total_peptides, own_rows), 0)

time: 85.3 us -> 89.4 us (1.048)
  matrix products: 16.4 us -> 19.9 us
  local copies, waits for them, and re-layouts: 42.3 us -> 43.5 us
    dot_general x1, matrix products: 13.3 us -> 16.8 us  [local(): jnp.einsum('mb,sb->ms', copies, corrected, preferred_element_type=jnp.flo...]
    unnamed x11 -> x20, local copies, waits for them, and re-layouts: 2.71 us -> 3.81 us
    dot_general x2 -> x1, local copies, waits for them, and re-layouts: 3.95 us -> 3.71 us  [local(): jnp.einsum('mb,sb->ms', copies, corrected, preferred_element_type=jnp.flo...]
where the time goes in v1:
time: 89.4 us; the launch traced here: 89 us
  local copies, waits for them, and re-layouts  43.5 us (49%)
  matrix products  19.9 us (22%)
  blocking collectives  12 us (13%)
  waiting for transfers between devices  5.51 us (6%)
  starting transfers between devices  4.87 us (5%)
  other arithmetic  2.27 us (3%)
    gather x48, local copies, waits for them, and re-layouts  33.9 us
    dot_general x1, matrix products, local(): jnp.einsum('mb,sb->ms', copies, corrected, preferred_element_type=jnp.flo...  16.8 us
    all_gather x1, blocking collectives, local(): piece = lax.all_gather(theo, 'band', axis=1, tiled=True)  12 us
    all_to_all x1, waiting for transfers between devices, local(): tiles = lax.all_to_all(tiles, 'query', split_axis=0, concat_axis=0)  5.51 us
    all_to_all x1, starting transfers between devices, local(): tiles = lax.all_to_all(tiles, 'query', split_axis=0, concat_axis=0)  4.87 us
    unnamed x20, local copies, waits for them, and re-layouts  3.81 us
    dot_general x1, local copies, waits for them, and re-layouts, local(): jnp.einsum('mb,sb->ms', copies, corrected, preferred_element_type=jnp.flo...  3.71 us
    dot_general x1, matrix products, correct(): jnp.einsum('rbj,ji->rbi', stacked, box_table(), preferred_element_type=jn...  3.08 us
  transfers between devices with their start and end apart: 1, of which 1 were waited for; matrix products, arithmetic and copies ran while one was open for 0% of the time, Pallas kernels for 0%

profile of v1, /device:TPU:0, one launch (start us, length us, event | category | flops | bytes accessed | tf_op | source)
XLA Modules:
  0.0 89.0 jit_solution(6712639845234634490)
XLA Ops:
  0.7 1.2 %copy.15 = bf16[1,2,20480]{2,0,1:T(2,128)(2,1)S(1)} copy(bf16[1,2,20480]{2,1,0:T(2,128)(2,1)} %param.6) | data formatting | bytes 163840 | tf_op args[1]
  1.8 12.0 %all_gather.3 = bf16[1,8,20480]{2,0,1:T(2,128)(2,1)S(1)} all-gather(bf16[1,2,20480]{2,0,1:T(2,128)(2,1)S(1)} %copy.15), channel_id=1, replica_groups=mesh['band'=4,'query'=8] {'band'}, dimensions={1}, use_global_device_ids=true | all-gather | bytes 409600 | tf_op jit(solution)/shard_map/all_gather | solution.py:50
  13.8 0.4 copy.33
  14.2 0.7 fusion.35
  14.9 34.0 %while.1 = (s32[]{:T(128)}, bf16[8,20736]{1,0:T(8,128)(2,1)S(1)}, s32[16,2]{0,1:T(2,128)S(1)}, bf16[16,8,20480]{2,1,0:T(8,128)(2,1)}, s32[]{:T(128)}) while((s32[]{:T(128)}, bf16[8,20736]{1,0:T(8,128)(2,1)S(1)}, s32[16,2]{0,1:T(2,128)S(1)}, bf16[16,8,20480]{2,1,0:T(8,128)(2,1)}, s32[]{:T(128)}) %tuple.25), condition=%wide.while_cond, body=%wide.while_body.sunk | while | flops 2 | bytes 655973 | solution.py:36
  14.9 0.1 constant_dynamic-slice_fusion.2
  15.0 0.5 slice.24
  15.5 1.5 %bitcast_dynamic-update-slice_fusion.2 = bf16[16,8,20480]{2,1,0:T(8,128)(2,1)} fusion(bf16[16,8,20480]{2,1,0:T(8,128)(2,1)} %get-tuple-element.60, s32[]{:T(128)S(6)} %copy.37, bf16[8,20736]{1,0:T(8,128)(2,1)S(1)} %get-tuple-element.63, s32[]{:T(128)} %bitcast.65), kind=kLoop, calls=%fused_computation.clone.1 | loop fusion | bytes 655876 | tf_op jit(solution)/shard_map/vmap()/gather
  17.0 0.1 constant_dynamic-slice_fusion.2
  17.1 0.5 slice.24
  17.6 1.5 %bitcast_dynamic-update-slice_fusion.2 = bf16[16,8,20480]{2,1,0:T(8,128)(2,1)} fusion(bf16[16,8,20480]{2,1,0:T(8,128)(2,1)} %get-tuple-element.60, s32[]{:T(128)S(6)} %copy.37, bf16[8,20736]{1,0:T(8,128)(2,1)S(1)} %get-tuple-element.63, s32[]{:T(128)} %bitcast.65), kind=kLoop, calls=%fused_computation.clone.1 | loop fusion | bytes 655876 | tf_op jit(solution)/shard_map/vmap()/gather
  19.2 0.1 constant_dynamic-slice_fusion.2
  19.2 0.5 slice.24
  19.8 1.5 %bitcast_dynamic-update-slice_fusion.2 = bf16[16,8,20480]{2,1,0:T(8,128)(2,1)} fusion(bf16[16,8,20480]{2,1,0:T(8,128)(2,1)} %get-tuple-element.60, s32[]{:T(128)S(6)} %copy.37, bf16[8,20736]{1,0:T(8,128)(2,1)S(1)} %get-tuple-element.63, s32[]{:T(128)} %bitcast.65), kind=kLoop, calls=%fused_computation.clone.1 | loop fusion | bytes 655876 | tf_op jit(solution)/shard_map/vmap()/gather
  21.3 0.1 constant_dynamic-slice_fusion.2
  21.4 0.5 slice.24
  21.9 1.5 %bitcast_dynamic-update-slice_fusion.2 = bf16[16,8,20480]{2,1,0:T(8,128)(2,1)} fusion(bf16[16,8,20480]{2,1,0:T(8,128)(2,1)} %get-tuple-element.60, s32[]{:T(128)S(6)} %copy.37, bf16[8,20736]{1,0:T(8,128)(2,1)S(1)} %get-tuple-element.63, s32[]{:T(128)} %bitcast.65), kind=kLoop, calls=%fused_computation.clone.1 | loop fusion | bytes 655876 | tf_op jit(solution)/shard_map/vmap()/gather
  23.4 0.1 constant_dynamic-slice_fusion.2
  23.5 0.5 slice.24
  24.0 1.5 %bitcast_dynamic-update-slice_fusion.2 = bf16[16,8,20480]{2,1,0:T(8,128)(2,1)} fusion(bf16[16,8,20480]{2,1,0:T(8,128)(2,1)} %get-tuple-element.60, s32[]{:T(128)S(6)} %copy.37, bf16[8,20736]{1,0:T(8,128)(2,1)S(1)} %get-tuple-element.63, s32[]{:T(128)} %bitcast.65), kind=kLoop, calls=%fused_computation.clone.1 | loop fusion | bytes 655876 | tf_op jit(solution)/shard_map/vmap()/gather
  25.5 0.1 constant_dynamic-slice_fusion.2
  25.6 0.5 slice.24
  26.1 1.5 %bitcast_dynamic-update-slice_fusion.2 = bf16[16,8,20480]{2,1,0:T(8,128)(2,1)} fusion(bf16[16,8,20480]{2,1,0:T(8,128)(2,1)} %get-tuple-element.60, s32[]{:T(128)S(6)} %copy.37, bf16[8,20736]{1,0:T(8,128)(2,1)S(1)} %get-tuple-element.63, s32[]{:T(128)} %bitcast.65), kind=kLoop, calls=%fused_computation.clone.1 | loop fusion | bytes 655876 | tf_op jit(solution)/shard_map/vmap()/gather
  27.7 0.1 constant_dynamic-slice_fusion.2
  27.7 0.5 slice.24
  28.2 1.6 %bitcast_dynamic-update-slice_fusion.2 = bf16[16,8,20480]{2,1,0:T(8,128)(2,1)} fusion(bf16[16,8,20480]{2,1,0:T(8,128)(2,1)} %get-tuple-element.60, s32[]{:T(128)S(6)} %copy.37, bf16[8,20736]{1,0:T(8,128)(2,1)S(1)} %get-tuple-element.63, s32[]{:T(128)} %bitcast.65), kind=kLoop, calls=%fused_computation.clone.1 | loop fusion | bytes 655876 | tf_op jit(solution)/shard_map/vmap()/gather
  29.8 0.1 constant_dynamic-slice_fusion.2
  29.9 0.5 slice.24
  30.4 1.5 %bitcast_dynamic-update-slice_fusion.2 = bf16[16,8,20480]{2,1,0:T(8,128)(2,1)} fusion(bf16[16,8,20480]{2,1,0:T(8,128)(2,1)} %get-tuple-element.60, s32[]{:T(128)S(6)} %copy.37, bf16[8,20736]{1,0:T(8,128)(2,1)S(1)} %get-tuple-element.63, s32[]{:T(128)} %bitcast.65), kind=kLoop, calls=%fused_computation.clone.1 | loop fusion | bytes 655876 | tf_op jit(solution)/shard_map/vmap()/gather
  31.9 0.1 constant_dynamic-slice_fusion.2
  32.0 0.5 slice.24
  32.5 1.5 %bitcast_dynamic-update-slice_fusion.2 = bf16[16,8,20480]{2,1,0:T(8,128)(2,1)} fusion(bf16[16,8,20480]{2,1,0:T(8,128)(2,1)} %get-tuple-element.60, s32[]{:T(128)S(6)} %copy.37, bf16[8,20736]{1,0:T(8,128)(2,1)S(1)} %get-tuple-element.63, s32[]{:T(128)} %bitcast.65), kind=kLoop, calls=%fused_computation.clone.1 | loop fusion | bytes 655876 | tf_op jit(solution)/shard_map/vmap()/gather
  34.0 0.1 constant_dynamic-slice_fusion.2
  34.1 0.5 slice.24
  34.6 1.5 %bitcast_dynamic-update-slice_fusion.2 = bf16[16,8,20480]{2,1,0:T(8,128)(2,1)} fusion(bf16[16,8,20480]{2,1,0:T(8,128)(2,1)} %get-tuple-element.60, s32[]{:T(128)S(6)} %copy.37, bf16[8,20736]{1,0:T(8,128)(2,1)S(1)} %get-tuple-element.63, s32[]{:T(128)} %bitcast.65), kind=kLoop, calls=%fused_computation.clone.1 | loop fusion | bytes 655876 | tf_op jit(solution)/shard_map/vmap()/gather
  36.2 0.5 slice.24
  36.8 1.5 %bitcast_dynamic-update-slice_fusion.2 = bf16[16,8,20480]{2,1,0:T(8,128)(2,1)} fusion(bf16[16,8,20480]{2,1,0:T(8,128)(2,1)} %get-tuple-element.60, s32[]{:T(128)S(6)} %copy.37, bf16[8,20736]{1,0:T(8,128)(2,1)S(1)} %get-tuple-element.63, s32[]{:T(128)} %bitcast.65), kind=kLoop, calls=%fused_computation.clone.1 | loop fusion | bytes 655876 | tf_op jit(solution)/shard_map/vmap()/gather
  38.4 0.5 slice.24
  38.9 1.5 %bitcast_dynamic-update-slice_fusion.2 = bf16[16,8,20480]{2,1,0:T(8,128)(2,1)} fusion(bf16[16,8,20480]{2,1,0:T(8,128)(2,1)} %get-tuple-element.60, s32[]{:T(128)S(6)} %copy.37, bf16[8,20736]{1,0:T(8,128)(2,1)S(1)} %get-tuple-element.63, s32[]{:T(128)} %bitcast.65), kind=kLoop, calls=%fused_computation.clone.1 | loop fusion | bytes 655876 | tf_op jit(solution)/shard_map/vmap()/gather
  40.5 0.5 slice.24
  41.0 1.5 %bitcast_dynamic-update-slice_fusion.2 = bf16[16,8,20480]{2,1,0:T(8,128)(2,1)} fusion(bf16[16,8,20480]{2,1,0:T(8,128)(2,1)} %get-tuple-element.60, s32[]{:T(128)S(6)} %copy.37, bf16[8,20736]{1,0:T(8,128)(2,1)S(1)} %get-tuple-element.63, s32[]{:T(128)} %bitcast.65), kind=kLoop, calls=%fused_computation.clone.1 | loop fusion | bytes 655876 | tf_op jit(solution)/shard_map/vmap()/gather
  42.6 0.5 slice.24
  43.1 1.5 %bitcast_dynamic-update-slice_fusion.2 = bf16[16,8,20480]{2,1,0:T(8,128)(2,1)} fusion(bf16[16,8,20480]{2,1,0:T(8,128)(2,1)} %get-tuple-element.60, s32[]{:T(128)S(6)} %copy.37, bf16[8,20736]{1,0:T(8,128)(2,1)S(1)} %get-tuple-element.63, s32[]{:T(128)} %bitcast.65), kind=kLoop, calls=%fused_computation.clone.1 | loop fusion | bytes 655876 | tf_op jit(solution)/shard_map/vmap()/gather
  44.7 0.5 slice.24
  45.2 1.5 %bitcast_dynamic-update-slice_fusion.2 = bf16[16,8,20480]{2,1,0:T(8,128)(2,1)} fusion(bf16[16,8,20480]{2,1,0:T(8,128)(2,1)} %get-tuple-element.60, s32[]{:T(128)S(6)} %copy.37, bf16[8,20736]{1,0:T(8,128)(2,1)S(1)} %get-tuple-element.63, s32[]{:T(128)} %bitcast.65), kind=kLoop, calls=%fused_computation.clone.1 | loop fusion | bytes 655876 | tf_op jit(solution)/shard_map/vmap()/gather
  46.8 0.5 slice.24
  47.3 1.5 %bitcast_dynamic-update-slice_fusion.2 = bf16[16,8,20480]{2,1,0:T(8,128)(2,1)} fusion(bf16[16,8,20480]{2,1,0:T(8,128)(2,1)} %get-tuple-element.60, s32[]{:T(128)S(6)} %copy.37, bf16[8,20736]{1,0:T(8,128)(2,1)S(1)} %get-tuple-element.63, s32[]{:T(128)} %bitcast.65), kind=kLoop, calls=%fused_computation.clone.1 | loop fusion | bytes 655876 | tf_op jit(solution)/shard_map/vmap()/gather
  48.9 0.3 copy.27
  49.2 1.2 %fusion.42 = (bf16[48,159,128]{2,1,0:T(8,128)(2,1)S(1)}, bf16[48,159,128]{2,1,0:T(8,128)(2,1)S(1)}) fusion(bf16[48,160,128]{2,1,0:T(8,128)(2,1)S(1)} %bitcast.66), kind=kLoop, calls=%fused_computation.61 | loop fusion | bytes 7815168 | tf_op jit(solution)/shard_map/slice | solution.py:23
  50.4 3.1 %subtract_convert_fusion = bf16[48,160,128]{2,1,0:T(8,128)(2,1)} fusion(bf16[48,160,128]{2,1,0:T(8,128)(2,1)S(1)} %bitcast.67, bf16[48,159,128]{2,1,0:T(8,128)(2,1)S(1)} %get-tuple-element.25, bf16[48,159,128]{2,1,0:T(8,128)(2,1)S(1)} %get-tuple-element.24, s32[384]{0:T(512)S(1)} %iota_add_fusion), kind=kOutput, calls=%fused_computation.16 | convolution fusion | flops 788643840 | bytes 7841280 | tf_op jit(solution)/shard_map/rbj,ji->rbi/dot_general | solution.py:26
  53.5 3.7 %dot_general.9 = bf16[8,6,20480]{2,1,0:T(8,128)(2,1)S(1)} reshape(bf16[48,160,128]{2,1,0:T(8,128)(2,1)} %subtract_convert_fusion) | data formatting | bytes 3932160 | tf_op jit(solution)/shard_map/mb,sb->ms/dot_general | solution.py:53
  57.3 16.8 %fusion.12 = f32[8,16,8,6]{0,2,3,1:T(8,128)S(1)} fusion(bf16[16,8,20480]{2,1,0:T(8,128)(2,1)} %get-tuple-element.9, bf16[8,6,20480]{2,1,0:T(8,128)(2,1)S(1)} %dot_general.9), kind=kOutput, calls=%fused_computation.14 | convolution fusion | flops 251658240 | bytes 7233536 | tf_op jit(solution)/shard_map/mb,sb->ms/dot_general | solution.py:53
  74.5 0.3 copy.17
  74.8 0.7 reshape.72
  75.5 4.9 %all-to-all-start = ((f32[8,1,768]{2,1,0:T(1,128)}), f32[8,1,768]{2,1,0:T(1,128)S(1)}, u32[]{:S(2)}, u32[]{:S(2)}) async-start(f32[8,1,768]{2,1,0:T(1,128)} %reshape.72), calls=%async_computation | async-start | bytes 49152 | tf_op jit(solution)/shard_map/all_to_all | solution.py:60
  80.5 0.1 dynamic-slice_add_fusion
  80.5 0.1 compare_and_fusion
  80.6 5.5 %all-to-all-done = f32[8,1,768]{2,1,0:T(1,128)S(1)} async-done(((f32[8,1,768]{2,1,0:T(1,128)}), f32[8,1,768]{2,1,0:T(1,128)S(1)}, u32[]{:S(2)}, u32[]{:S(2)}) %all-to-all-start) | async-done | bytes 24608 | tf_op jit(solution)/shard_map/all_to_all | solution.py:60
  86.1 0.5 broadcast.91
  86.6 0.7 reduce.2
  87.3 0.1 reshape.73
  87.5 0.7 select_reduce_fusion
  88.2 0.1 copy.25
  88.3 0.7 copy.21
  (26 shorter events, 0.9 us)
Async XLA Ops:
  0.6 48.3 %copy-start = (bf16[48,20480]{1,0:T(8,128)(2,1)S(1)}, bf16[48,20480]{1,0:T(8,128)(2,1)}, u32[]{:S(2)}) copy-start(bf16[48,20480]{1,0:T(8,128)(2,1)} %param.5) | copy-start | bytes 5898244
  57.2 23.2 %copy-start.1 = (s32[48]{0:T(128)S(1)}, s32[48]{0:T(128)}, u32[]{:S(2)}) copy-start(s32[48]{0:T(128)} %param.9) | copy-start | bytes 580
  57.3 23.2 %copy-start.2 = (s32[48]{0:T(128)S(1)}, s32[48]{0:T(128)}, u32[]{:S(2)}) copy-start(s32[48]{0:T(128)} %param.8) | copy-start | bytes 580
  75.5 10.6 %all-to-all-start = ((f32[8,1,768]{2,1,0:T(1,128)}), f32[8,1,768]{2,1,0:T(1,128)S(1)}, u32[]{:S(2)}, u32[]{:S(2)}) async-start(f32[8,1,768]{2,1,0:T(1,128)} %reshape.72), calls=%async_computation | async-start | bytes 49152 | tf_op jit(solution)/shard_map/all_to_all | solution.py:60
